TPU v7x, 256 devices: a whole 4x4x8 slice. The times are simulated.
256 devices in a mesh: dp: 32 (over z_hi, y, core), expert: 8 (over x, z_lo).
Axes of the slice: x: 4, y: 4, z: 8 (z_hi: 4, z_lo: 2; z = z_hi * 2 + z_lo), core: 2. Of those that a mesh axis runs over, the one named last changes fastest.
Arguments:
- tokens: bfloat16 [49152, 2048], P(('dp', 'expert')), may hold values from -24 to 24
- routes: int32 [49152, 6], P(('dp', 'expert')), may hold values from 0 to 63, as said below
- gate_scale: float32 [49152, 6], P(('dp', 'expert')), may hold values from 0.2 to 2
- w_gate: bfloat16 [8, 2048, 768], P('expert', 'dp'), may hold values from -0.125 to 0.125
- w_up: bfloat16 [8, 2048, 768], P('expert', 'dp'), may hold values from -0.125 to 0.125
- w_down: bfloat16 [8, 2048, 768], P('expert', 'dp'), may hold values from -0.21875 to 0.21875
- d_out: bfloat16 [49152, 2048], P(('dp', 'expert')), may hold values from -24 to 24
Outputs:
- layer_out: bfloat16 [49152, 2048], P(('dp', 'expert'))
- d_tokens: bfloat16 [49152, 2048], P(('dp', 'expert'))
- grad_gate: float32 [8, 2048, 768], P('expert', 'dp')
- grad_up: float32 [8, 2048, 768], P('expert', 'dp')
- grad_down: float32 [8, 2048, 768], P('expert', 'dp')
Inputs may be any that keep to these rules, and one draw needn't show every extreme that they name: `routes`: each token names 6 different experts. The experts of this window are 0 to 7; among the 192 tokens of one device no window expert is named by more than 32 tokens.
All inputs are finite; a program needn't handle non-finite values.
Results may differ from a plain program's by a relative error of at most 0.02.
Values may be sent and summed in bfloat16 or wider, within the bound.
A program may use at most 64 MiB of HBM per device.

v0:
```python
import jax
import jax.numpy as jnp
from jax import lax
from jax.sharding import PartitionSpec as P

CAP = 32


def shards(tokens, routes, gate_scale, w_gate, w_up, w_down, d_out):
    experts_here = lax.axis_size("expert")
    tok_count = tokens.shape[0]
    width = tokens.shape[1]
    choices_per = routes.shape[1]
    capacity = CAP
    slots = experts_here * capacity
    flat_count = tok_count * choices_per
    combine = gate_scale / jnp.sum(gate_scale, axis=1, keepdims=True)
    flat_ids = routes.reshape(flat_count)
    flat_weight = combine.reshape(flat_count)
    live = flat_ids < experts_here
    onehot = (
        (flat_ids[:, None] == jnp.arange(experts_here, dtype=jnp.int32)[None, :]) & live[:, None]
    ).astype(jnp.int32)
    position = jnp.sum((jnp.cumsum(onehot, axis=0) - onehot) * onehot, axis=1)
    dest = jnp.where(live, flat_ids * capacity + position, slots)
    match = jnp.arange(slots, dtype=jnp.int32)[:, None] == dest[None, :]
    filled = jnp.any(match, axis=1)
    owner = jnp.sum(
        jnp.where(match, (jnp.arange(flat_count, dtype=jnp.int32) // choices_per)[None, :], 0),
        axis=1,
    )
    slot_weight = jnp.sum(jnp.where(match, flat_weight[None, :], 0.0), axis=1)
    send_x = jnp.where(filled[:, None], tokens[owner], jnp.zeros((), jnp.bfloat16))
    send_d = jnp.where(
        filled[:, None], d_out[owner].astype(jnp.float32) * slot_weight[:, None], 0.0
    ).astype(jnp.bfloat16)
    send_x = send_x.reshape(experts_here, capacity, width)
    send_d = send_d.reshape(experts_here, capacity, width)
    full_gate, full_up, full_down = (
        lax.all_gather(w_gate, "dp", axis=1, tiled=True),
        lax.all_gather(w_up, "dp", axis=1, tiled=True),
        lax.all_gather(w_down, "dp", axis=1, tiled=True),
    )
    recv_x, recv_d = (
        lax.all_to_all(send_x, "expert", split_axis=0, concat_axis=0, tiled=True),
        lax.all_to_all(send_d, "expert", split_axis=0, concat_axis=0, tiled=True),
    )
    weight_gate = full_gate[0]
    weight_up = full_up[0]
    weight_down = full_down[0]
    rows_x = recv_x.reshape(slots, width)
    rows_d = recv_d.reshape(slots, width)
    contract_last = (((1,), (1,)), ((), ()))
    contract_first = (((0,), (0,)), ((), ()))
    gate = jnp.dot(rows_x, weight_gate, preferred_element_type=jnp.float32)
    up = jnp.dot(rows_x, weight_up, preferred_element_type=jnp.float32)
    sig = jax.nn.sigmoid(gate)
    act = gate * sig
    hidden = (act * up).astype(jnp.bfloat16)
    expert_out = lax.dot_general(
        hidden, weight_down, contract_last, preferred_element_type=jnp.float32
    ).astype(jnp.bfloat16)
    d_hidden = jnp.dot(rows_d, weight_down, preferred_element_type=jnp.float32)
    d_gate = (d_hidden * up * sig * (1.0 + gate * (1.0 - sig))).astype(jnp.bfloat16)
    d_up = (d_hidden * act).astype(jnp.bfloat16)
    d_in = (
        lax.dot_general(d_gate, weight_gate, contract_last, preferred_element_type=jnp.float32)
        + lax.dot_general(d_up, weight_up, contract_last, preferred_element_type=jnp.float32)
    ).astype(jnp.bfloat16)
    back_out, back_in = (
        lax.all_to_all(
            expert_out.reshape(experts_here, capacity, width),
            "expert",
            split_axis=0,
            concat_axis=0,
            tiled=True,
        ),
        lax.all_to_all(
            d_in.reshape(experts_here, capacity, width),
            "expert",
            split_axis=0,
            concat_axis=0,
            tiled=True,
        ),
    )
    term_gate = lax.dot_general(rows_x, d_gate, contract_first, preferred_element_type=jnp.float32)
    term_up = lax.dot_general(rows_x, d_up, contract_first, preferred_element_type=jnp.float32)
    term_down = lax.dot_general(rows_d, hidden, contract_first, preferred_element_type=jnp.float32)
    grad_gate, grad_up, grad_down = (
        lax.psum_scatter(
            term_gate.astype(jnp.bfloat16), "dp", scatter_dimension=0, tiled=True
        ).astype(jnp.float32),
        lax.psum_scatter(
            term_up.astype(jnp.bfloat16), "dp", scatter_dimension=0, tiled=True
        ).astype(jnp.float32),
        lax.psum_scatter(
            term_down.astype(jnp.bfloat16), "dp", scatter_dimension=0, tiled=True
        ).astype(jnp.float32),
    )
    back_out = back_out.reshape(slots, width)
    back_in = back_in.reshape(slots, width)
    dest_tok = dest.reshape(tok_count, choices_per)
    live_tok = live.reshape(tok_count, choices_per)
    weight_tok = jnp.where(live_tok, combine, 0.0)
    safe_rows = jnp.where(live_tok, dest_tok, 0)
    total_out = jnp.zeros((tok_count, width), jnp.float32)
    total_in = jnp.zeros((tok_count, width), jnp.float32)
    for choice_index in range(choices_per):
        rows_pick = safe_rows[:, choice_index]
        total_out = total_out + weight_tok[:, choice_index : choice_index + 1] * back_out[
            rows_pick
        ].astype(jnp.float32)
        total_in = total_in + jnp.where(
            live_tok[:, choice_index : choice_index + 1],
            back_in[rows_pick].astype(jnp.float32),
            0.0,
        )
    layer_out = total_out.astype(jnp.bfloat16)
    d_tokens = total_in.astype(jnp.bfloat16)
    return (layer_out, d_tokens, grad_gate[None], grad_up[None], grad_down[None])


def solution(mesh):
    placed = (
        P(("dp", "expert"), None),
        P(("dp", "expert"), None),
        P(("dp", "expert"), None),
        P("expert", "dp", None),
        P("expert", "dp", None),
        P("expert", "dp", None),
        P(("dp", "expert"), None),
    )
    return jax.shard_map(
        shards,
        mesh=mesh,
        in_specs=placed,
        out_specs=(
            P(("dp", "expert"), None),
            P(("dp", "expert"), None),
            P("expert", "dp", None),
            P("expert", "dp", None),
            P("expert", "dp", None),
        ),
        check_vma=False,
    )
```

profile of v0, /device:TPU:2, one launch (start us, length us, event | category | flops | bytes accessed | tf_op | source)
XLA Modules:
  0.0 494.1 jit_solution(7565816909941220168)
XLA Ops:
  9.4 0.8 copy.30
  10.5 2.3 reduce-window.6
  16.0 1.4 gather_fusion.7
  17.3 1.3 fusion.22
  18.6 6.3 %all-to-all-start.2 = ((bf16[8,32,2048]{2,1,0:T(8,128)(2,1)}), bf16[8,32,2048]{2,1,0:T(8,128)(2,1)S(1)}, u32[]{:S(2)}, u32[]{:S(2)}) async-start(bf16[8,32,2048]{2,1,0:T(8,128)(2,1)} %fusion.22), calls=%async_computation.2 | async-start | bytes 2097152 | tf_op jit(solution)/shard_map/all_to_all | solution.py:46
  25.0 2.3 gather_fusion
  27.3 2.4 broadcast_select_fusion
  29.7 11.4 %all-to-all-done.2 = bf16[8,32,2048]{2,1,0:T(8,128)(2,1)S(1)} async-done(((bf16[8,32,2048]{2,1,0:T(8,128)(2,1)}), bf16[8,32,2048]{2,1,0:T(8,128)(2,1)S(1)}, u32[]{:S(2)}, u32[]{:S(2)}) %all-to-all-start.2) | async-done | bytes 1048608 | tf_op jit(solution)/shard_map/all_to_all | solution.py:46
  41.1 1.0 copy-done.2
  42.1 6.1 %all-to-all-start = ((bf16[8,32,2048]{2,1,0:T(8,128)(2,1)}), bf16[8,32,2048]{2,1,0:T(8,128)(2,1)S(1)}, u32[]{:S(2)}, u32[]{:S(2)}) async-start(bf16[8,32,2048]{2,1,0:T(8,128)(2,1)} %broadcast_select_fusion), calls=%async_computation | async-start | bytes 2097152 | tf_op jit(solution)/shard_map/all_to_all | solution.py:45
  48.3 27.3 %all-gather.8.cloned.1.call-done = bf16[1,2048,768]{2,1,0:T(8,128)(2,1)} async-done(((bf16[1,64,768]{2,1,0:T(8,128)(2,1)}), bf16[1,2048,768]{2,1,0:T(8,128)(2,1)}) %all-gather.8.cloned.1.call-update) | async-done | bytes 3145744 | tf_op jit(solution)/shard_map/all_gather | solution.py:42
  75.6 4.1 fusion
  79.6 52.9 %all-gather.6.cloned.1.call-done = bf16[1,2048,768]{2,1,0:T(8,128)(2,1)} async-done(((bf16[1,64,768]{2,1,0:T(8,128)(2,1)}), bf16[1,2048,768]{2,1,0:T(8,128)(2,1)}) %all-gather.6.cloned.1.call-update) | async-done | bytes 3145744 | tf_op jit(solution)/shard_map/all_gather | solution.py:41
  132.5 3.7 fusion.6
  136.2 53.7 %all-gather.4.cloned.1.call-done = bf16[1,2048,768]{2,1,0:T(8,128)(2,1)} async-done(((bf16[1,64,768]{2,1,0:T(8,128)(2,1)}), bf16[1,2048,768]{2,1,0:T(8,128)(2,1)}) %all-gather.4.cloned.1.call-update) | async-done | bytes 3145744 | tf_op jit(solution)/shard_map/all_gather | solution.py:40
  189.9 4.3 multiply_convert_fusion.1
  194.9 2.8 convolution_convert_fusion
  197.8 2.7 convolution_convert_fusion.2
  200.5 1.0 copy-done.12
  201.5 3.0 fusion.4
  204.5 2.1 fusion.15
  206.6 5.3 %all-to-all-start.3 = ((bf16[8,32,2048]{2,1,0:T(8,128)(2,1)}), bf16[8,32,2048]{2,1,0:T(8,128)(2,1)S(1)}, u32[]{:S(2)}, u32[]{:S(2)}) async-start(bf16[8,32,2048]{2,1,0:T(8,128)(2,1)} %bitcast.104), calls=%async_computation.3 | async-start | bytes 2097152 | tf_op jit(solution)/shard_map/all_to_all | solution.py:78
  212.0 2.7 convolution_convert_fusion.1
  214.7 1.0 copy-done.15
  215.7 3.9 fusion.18
  219.6 6.4 %all-to-all-done.3 = bf16[8,32,2048]{2,1,0:T(8,128)(2,1)S(1)} async-done(((bf16[8,32,2048]{2,1,0:T(8,128)(2,1)}), bf16[8,32,2048]{2,1,0:T(8,128)(2,1)S(1)}, u32[]{:S(2)}, u32[]{:S(2)}) %all-to-all-start.3) | async-done | bytes 1048608 | tf_op jit(solution)/shard_map/all_to_all | solution.py:78
  226.0 5.6 %all-to-all-start.1 = ((bf16[8,32,2048]{2,1,0:T(8,128)(2,1)}), bf16[8,32,2048]{2,1,0:T(8,128)(2,1)S(1)}, u32[]{:S(2)}, u32[]{:S(2)}) async-start(bf16[8,32,2048]{2,1,0:T(8,128)(2,1)} %bitcast.107), calls=%async_computation.1 | async-start | bytes 2097152 | tf_op jit(solution)/shard_map/all_to_all | solution.py:71
  232.0 2.0 gather_fusion.13
  234.0 10.8 %all-to-all-done.1 = bf16[8,32,2048]{2,1,0:T(8,128)(2,1)S(1)} async-done(((bf16[8,32,2048]{2,1,0:T(8,128)(2,1)}), bf16[8,32,2048]{2,1,0:T(8,128)(2,1)S(1)}, u32[]{:S(2)}, u32[]{:S(2)}) %all-to-all-start.1) | async-done | bytes 1048608 | tf_op jit(solution)/shard_map/all_to_all | solution.py:71
  244.8 2.0 gather_fusion.6
  246.9 2.0 gather_fusion.12
  248.9 2.0 gather_fusion.5
  250.9 2.0 gather_fusion.11
  252.9 2.1 gather_fusion.4
  255.0 2.0 gather_fusion.10
  257.0 2.0 gather_fusion.3
  259.1 2.1 gather_fusion.8
  261.1 2.0 gather_fusion.1
  263.2 2.1 gather_fusion.9
  265.2 2.1 gather_fusion.2
  267.3 4.1 add_convert_fusion
  271.5 1.9 add_convert_fusion.1
  273.3 18.0 %reduce-scatter.8.cloned.1.call-done = bf16[64,768]{1,0:T(8,128)(2,1)} async-done(((bf16[2048,768]{1,0:T(8,128)(2,1)}), bf16[64,768]{1,0:T(8,128)(2,1)}) %reduce-scatter.8.cloned.1.call-update) | async-done | bytes 98320 | tf_op jit(solution)/shard_map/reduce_scatter | solution.py:96
  291.3 1.6 bitcast_convert_fusion
  292.9 95.8 %reduce-scatter.4.cloned.1.call-done = bf16[64,768]{1,0:T(8,128)(2,1)} async-done(((bf16[2048,768]{1,0:T(8,128)(2,1)}), bf16[64,768]{1,0:T(8,128)(2,1)}) %reduce-scatter.4.cloned.1.call-update) | async-done | bytes 98320 | tf_op jit(solution)/shard_map/reduce_scatter | solution.py:90
  388.7 1.6 bitcast_convert_fusion.2
  390.3 95.4 %reduce-scatter.6.cloned.1.call-done = bf16[64,768]{1,0:T(8,128)(2,1)} async-done(((bf16[2048,768]{1,0:T(8,128)(2,1)}), bf16[64,768]{1,0:T(8,128)(2,1)}) %reduce-scatter.6.cloned.1.call-update) | async-done | bytes 98320 | tf_op jit(solution)/shard_map/reduce_scatter | solution.py:93
  485.6 1.6 bitcast_convert_fusion.1
  (77 shorter events, 6.8 us)
Async XLA Ops:
  7.2 8.8 %copy-start = (bf16[192,2048]{1,0:T(8,128)(2,1)S(1)}, bf16[192,2048]{1,0:T(8,128)(2,1)}, u32[]{:S(2)}) copy-start(bf16[192,2048]{1,0:T(8,128)(2,1)} %param.13) | copy-start | bytes 2359300
  7.2 68.4 %all-gather.8.cloned.1.call-start = ((), (), s32[]{:S(2)}) async-start(), calls=%async_computation.9 | async-start | bytes 3244032 | tf_op jit(solution)/shard_map/all_gather | solution.py:42
  7.9 124.6 %all-gather.6.cloned.1.call-start = ((), (), s32[]{:S(2)}) async-start(), calls=%async_computation.8 | async-start | bytes 3244032 | tf_op jit(solution)/shard_map/all_gather | solution.py:41
  8.7 181.2 %all-gather.4.cloned.1.call-start = ((), (), s32[]{:S(2)}) async-start(), calls=%async_computation.7 | async-start | bytes 3244032 | tf_op jit(solution)/shard_map/all_gather | solution.py:40
  18.6 6.3 %copy-start.1 = (bf16[192,2048]{1,0:T(8,128)(2,1)S(1)}, bf16[192,2048]{1,0:T(8,128)(2,1)}, u32[]{:S(2)}) copy-start(bf16[192,2048]{1,0:T(8,128)(2,1)} %param.7) | copy-start | bytes 2359300
  18.6 22.5 %all-to-all-start.2 = ((bf16[8,32,2048]{2,1,0:T(8,128)(2,1)}), bf16[8,32,2048]{2,1,0:T(8,128)(2,1)S(1)}, u32[]{:S(2)}, u32[]{:S(2)}) async-start(bf16[8,32,2048]{2,1,0:T(8,128)(2,1)} %fusion.22), calls=%async_computation.2 | async-start | bytes 2097152 | tf_op jit(solution)/shard_map/all_to_all | solution.py:46
  41.1 1.0 copy-start.2
  42.1 37.5 %all-to-all-start = ((bf16[8,32,2048]{2,1,0:T(8,128)(2,1)}), bf16[8,32,2048]{2,1,0:T(8,128)(2,1)S(1)}, u32[]{:S(2)}, u32[]{:S(2)}) async-start(bf16[8,32,2048]{2,1,0:T(8,128)(2,1)} %broadcast_select_fusion), calls=%async_computation | async-start | bytes 2097152 | tf_op jit(solution)/shard_map/all_to_all | solution.py:45
  48.3 243.1 %reduce-scatter.8.cloned.1.call-start = ((), (), s32[]{:S(2)}) async-start(), calls=%async_computation.12 | async-start | bytes 3244032 | tf_op jit(solution)/shard_map/reduce_scatter | solution.py:96
  136.2 58.7 %copy-start.3 = (bf16[8,32,2048]{2,1,0:T(8,128)(2,1)S(1)}, bf16[8,32,2048]{2,1,0:T(8,128)(2,1)}, u32[]{:S(2)}) copy-start(bf16[8,32,2048]{2,1,0:T(8,128)(2,1)} %copy-done.2) | copy-start | bytes 3145732
  194.2 0.7 copy-start.14
  197.7 191.0 %reduce-scatter.4.cloned.1.call-start = ((), (), s32[]{:S(2)}) async-start(), calls=%async_computation.10 | async-start | bytes 3244032 | tf_op jit(solution)/shard_map/reduce_scatter | solution.py:90
  200.5 1.0 copy-start.12
  201.5 3.1 copy-start.4
  206.6 5.3 %copy-start.13 = (bf16[256,768]{1,0:T(8,128)(2,1)S(1)}, bf16[256,768]{1,0:T(8,128)(2,1)}, u32[]{:S(2)}) copy-start(bf16[256,768]{1,0:T(8,128)(2,1)} %get-tuple-element.15) | copy-start | bytes 1179652
  206.6 19.4 %all-to-all-start.3 = ((bf16[8,32,2048]{2,1,0:T(8,128)(2,1)}), bf16[8,32,2048]{2,1,0:T(8,128)(2,1)S(1)}, u32[]{:S(2)}, u32[]{:S(2)}) async-start(bf16[8,32,2048]{2,1,0:T(8,128)(2,1)} %bitcast.104), calls=%async_computation.3 | async-start | bytes 2097152 | tf_op jit(solution)/shard_map/all_to_all | solution.py:78
  212.0 273.7 %reduce-scatter.6.cloned.1.call-start = ((), (), s32[]{:S(2)}) async-start(), calls=%async_computation.11 | async-start | bytes 3244032 | tf_op jit(solution)/shard_map/reduce_scatter | solution.py:93
  214.7 1.0 copy-start.15
  219.6 12.2 %copy-start.16 = (s32[192,6]{0,1:T(8,128)S(1)}, s32[192,6]{0,1:T(8,128)}, u32[]{:S(2)}) copy-start(s32[192,6]{0,1:T(8,128)} %param.8) | copy-start | bytes 13828
  226.0 18.8 %all-to-all-start.1 = ((bf16[8,32,2048]{2,1,0:T(8,128)(2,1)}), bf16[8,32,2048]{2,1,0:T(8,128)(2,1)S(1)}, u32[]{:S(2)}, u32[]{:S(2)}) async-start(bf16[8,32,2048]{2,1,0:T(8,128)(2,1)} %bitcast.107), calls=%async_computation.1 | async-start | bytes 2097152 | tf_op jit(solution)/shard_map/all_to_all | solution.py:71
  265.2 2.1 copy-start.9
  267.3 4.1 copy-start.5
  267.3 4.1 copy-start.6
  267.3 4.1 copy-start.7
  267.3 4.1 copy-start.8
  267.3 4.1 copy-start.10
  267.3 4.1 copy-start.11
Sparse Core Ops, SparseCore 0:
  10.6 64.9 all-gather.7
  78.1 54.3 all-gather.5
  135.1 54.8 all-gather.3
  197.8 93.4 reduce-scatter.7
  295.6 93.0 reduce-scatter.3
  392.5 93.1 reduce-scatter.5
where the time goes:
time: 495 us; the launch traced here: 494 us
  waiting for transfers between devices  374 us (76%)
  local copies, waits for them, and re-layouts  33.9 us (7%)
  matrix products  29.4 us (6%)
  starting transfers between devices  23.5 us (5%)
  other arithmetic  19.1 us (4%)
  between operations  14.4 us (3%)
    reduce_scatter x1, waiting for transfers between devices, shards(): lax.psum_scatter(term_gate.astype(jnp.bfloat16), 'dp', scatter_dimension=...  95.8 us
    reduce_scatter x1, waiting for transfers between devices, shards(): lax.psum_scatter(term_up.astype(jnp.bfloat16), 'dp', scatter_dimension=0,...  95.4 us
    all_gather x1, waiting for transfers between devices, shards(): lax.all_gather(w_gate, 'dp', axis=1, tiled=True)  53.7 us
    all_gather x1, waiting for transfers between devices, shards(): lax.all_gather(w_up, 'dp', axis=1, tiled=True)  52.9 us
    all_gather x1, waiting for transfers between devices, shards(): lax.all_gather(w_down, 'dp', axis=1, tiled=True)  27.3 us
    reduce_scatter x1, waiting for transfers between devices, shards(): lax.psum_scatter(term_down.astype(jnp.bfloat16), 'dp', scatter_dimension=...  18 us
    gather x6, local copies, waits for them, and re-layouts, shards(): back_out[rows_pick].astype(jnp.float32)  12.3 us
    gather x6, local copies, waits for them, and re-layouts, shards(): back_in[rows_pick].astype(jnp.float32)  12.2 us
  transfers between devices with their start and end apart: 10, of which 9 were waited for; matrix products, arithmetic and copies ran while one was open for 14% of the time, Pallas kernels for 0%

commit v1 on v0

--- a/solution.py
+++ b/solution.py
@@ -39,7 +39,9 @@
     full_gate, full_up, full_down = (
         lax.all_gather(w_gate, "dp", axis=1, tiled=True),
         lax.all_gather(w_up, "dp", axis=1, tiled=True),
-        lax.all_gather(w_down, "dp", axis=1, tiled=True),
+        jnp.concatenate(
+            lax.all_to_all(jnp.stack([w_down] * lax.axis_size("dp")), "dp", 0, 0), axis=1
+        ),
     )
     recv_x, recv_d = (
         lax.all_to_all(send_x, "expert", split_axis=0, concat_axis=0, tiled=True),

time: 495 us -> 478 us (0.966)
  waiting for transfers between devices: 374 us -> 331 us
  blocking collectives: 0 us -> 22.1 us
  starting transfers between devices: 23.5 us -> 28.7 us
    reduce_scatter x1, waiting for transfers between devices: 18 us -> 95.3 us  [shards(): lax.psum_scatter(term_down.astype(jnp.bfloat16), 'dp', scatter_dimension=...]
    reduce_scatter x1, waiting for transfers between devices: 95.4 us -> 20.4 us  [shards(): lax.psum_scatter(term_up.astype(jnp.bfloat16), 'dp', scatter_dimension=0,...]
    all_to_all x1, waiting for transfers between devices: 11.4 us -> 81.2 us  [shards(): lax.all_to_all(jnp.stack([w_down] * lax.axis_size('dp')), 'dp', 0, 0)]
    all_gather x1, waiting for transfers between devices: 52.9 us -> 0.01 us  [shards(): lax.all_gather(w_up, 'dp', axis=1, tiled=True)]
    all_gather x1, waiting for transfers between devices: 53.7 us -> 1.97 us  [shards(): lax.all_gather(w_gate, 'dp', axis=1, tiled=True)]
    all_gather x1 -> x0, waiting for transfers between devices: 27.3 us -> none  [shards(): lax.all_gather(w_down, 'dp', axis=1, tiled=True)]
    all_to_all x0 -> x1, blocking collectives: none -> 22.1 us  [shards(): lax.all_to_all(send_d, 'expert', split_axis=0, concat_axis=0, tiled=True)]
    all_to_all x1, waiting for transfers between devices: 0.01 us -> 19.2 us  [shards(): lax.all_to_all(send_x, 'expert', split_axis=0, concat_axis=0, tiled=True)]
  transfers between devices with their start and end apart: 10 -> 9, of which waited for: 9 -> 8; matrix products, arithmetic and copies ran while one was open for 14% -> 15% of each run, Pallas kernels for 0% -> 0%
where the time goes in v1:
time: 478 us; the launch traced here: 477 us
  waiting for transfers between devices  331 us (69%)
  local copies, waits for them, and re-layouts  34 us (7%)
  matrix products  29.1 us (6%)
  starting transfers between devices  28.7 us (6%)
  blocking collectives  22.1 us (5%)
  other arithmetic  17.9 us (4%)
  between operations  14.1 us (3%)
    reduce_scatter x1, waiting for transfers between devices, shards(): lax.psum_scatter(term_gate.astype(jnp.bfloat16), 'dp', scatter_dimension=...  95.9 us
    reduce_scatter x1, waiting for transfers between devices, shards(): lax.psum_scatter(term_down.astype(jnp.bfloat16), 'dp', scatter_dimension=...  95.3 us
    all_to_all x1, waiting for transfers between devices, shards(): lax.all_to_all(jnp.stack([w_down] * lax.axis_size('dp')), 'dp', 0, 0)  81.2 us
    all_to_all x1, blocking collectives, shards(): lax.all_to_all(send_d, 'expert', split_axis=0, concat_axis=0, tiled=True)  22.1 us
    reduce_scatter x1, waiting for transfers between devices, shards(): lax.psum_scatter(term_up.astype(jnp.bfloat16), 'dp', scatter_dimension=0,...  20.4 us
    all_to_all x1, waiting for transfers between devices, shards(): lax.all_to_all(send_x, 'expert', split_axis=0, concat_axis=0, tiled=True)  19.2 us
    gather x6, local copies, waits for them, and re-layouts, shards(): back_in[rows_pick].astype(jnp.float32)  12.3 us
    gather x6, local copies, waits for them, and re-layouts, shards(): back_out[rows_pick].astype(jnp.float32)  12.2 us
  transfers between devices with their start and end apart: 9, of which 8 were waited for; matrix products, arithmetic and copies ran while one was open for 15% of the time, Pallas kernels for 0%

profile of v1, /device:TPU:2, one launch (start us, length us, event | category | flops | bytes accessed | tf_op | source)
XLA Modules:
  0.0 477.4 jit_solution(9331348633105131189)
XLA Ops:
  7.9 0.8 copy.30
  9.6 0.7 broadcast_select_fusion.1
  10.3 2.3 reduce-window.6
  14.5 1.4 gather_fusion.7
  16.2 22.1 %all_to_all.25 = bf16[8,32,2048]{2,1,0:T(8,128)(2,1)S(1)} all-to-all(bf16[8,32,2048]{2,1,0:T(8,128)(2,1)S(1)} %fusion.15), channel_id=1, replica_groups=mesh['dp'=32,'expert'=8] {'expert'}, dimensions={0} | all-to-all | bytes 2097152 | tf_op jit(solution)/shard_map/all_to_all | solution.py:48
  38.3 2.0 stack.2
  40.3 11.9 %all-to-all-start.1 = ((bf16[32,1,64,768]{3,2,1,0:T(8,128)(2,1)}), bf16[32,1,64,768]{3,2,1,0:T(8,128)(2,1)}, u32[]{:S(2)}, u32[]{:S(2)}) async-start(bf16[32,1,64,768]{3,2,1,0:T(8,128)(2,1)} %stack.2), calls=%async_computation.1 | async-start | bytes 6291456 | tf_op jit(solution)/shard_map/all_to_all | solution.py:43
  53.0 2.3 gather_fusion
  55.3 2.3 broadcast_select_fusion
  57.7 81.2 %all-to-all-done.1 = bf16[32,1,64,768]{3,2,1,0:T(8,128)(2,1)} async-done(((bf16[32,1,64,768]{3,2,1,0:T(8,128)(2,1)}), bf16[32,1,64,768]{3,2,1,0:T(8,128)(2,1)}, u32[]{:S(2)}, u32[]{:S(2)}) %all-to-all-start.1) | async-done | bytes 3145760 | tf_op jit(solution)/shard_map/all_to_all | solution.py:43
  138.8 5.8 %all-to-all-start = ((bf16[8,32,2048]{2,1,0:T(8,128)(2,1)}), bf16[8,32,2048]{2,1,0:T(8,128)(2,1)S(1)}, u32[]{:S(2)}, u32[]{:S(2)}) async-start(bf16[8,32,2048]{2,1,0:T(8,128)(2,1)} %broadcast_select_fusion), calls=%async_computation | async-start | bytes 2097152 | tf_op jit(solution)/shard_map/all_to_all | solution.py:47
  144.7 3.7 fusion.28
  148.4 19.2 %all-to-all-done = bf16[8,32,2048]{2,1,0:T(8,128)(2,1)S(1)} async-done(((bf16[8,32,2048]{2,1,0:T(8,128)(2,1)}), bf16[8,32,2048]{2,1,0:T(8,128)(2,1)S(1)}, u32[]{:S(2)}, u32[]{:S(2)}) %all-to-all-start) | async-done | bytes 1048608 | tf_op jit(solution)/shard_map/all_to_all | solution.py:47
  167.6 3.8 fusion.2
  171.5 2.0 all-gather.3.cloned.1.call-done
  173.4 4.3 multiply_convert_fusion.1
  177.7 0.7 copy-done.11
  178.5 2.7 convolution_convert_fusion.1
  181.3 2.7 convolution_convert_fusion.2
  184.0 1.0 copy-done.12
  185.0 3.0 fusion
  188.0 2.1 fusion.11
  190.1 5.3 %all-to-all-start.4 = ((bf16[8,32,2048]{2,1,0:T(8,128)(2,1)}), bf16[8,32,2048]{2,1,0:T(8,128)(2,1)S(1)}, u32[]{:S(2)}, u32[]{:S(2)}) async-start(bf16[8,32,2048]{2,1,0:T(8,128)(2,1)} %bitcast.101), calls=%async_computation.4 | async-start | bytes 2097152 | tf_op jit(solution)/shard_map/all_to_all | solution.py:80
  195.4 2.8 convolution_convert_fusion
  198.2 3.9 convolution_convert_fusion.3
  202.2 7.3 %all-to-all-done.4 = bf16[8,32,2048]{2,1,0:T(8,128)(2,1)S(1)} async-done(((bf16[8,32,2048]{2,1,0:T(8,128)(2,1)}), bf16[8,32,2048]{2,1,0:T(8,128)(2,1)S(1)}, u32[]{:S(2)}, u32[]{:S(2)}) %all-to-all-start.4) | async-done | bytes 1048608 | tf_op jit(solution)/shard_map/all_to_all | solution.py:80
  209.5 5.6 %all-to-all-start.2 = ((bf16[8,32,2048]{2,1,0:T(8,128)(2,1)}), bf16[8,32,2048]{2,1,0:T(8,128)(2,1)S(1)}, u32[]{:S(2)}, u32[]{:S(2)}) async-start(bf16[8,32,2048]{2,1,0:T(8,128)(2,1)} %bitcast.104), calls=%async_computation.2 | async-start | bytes 2097152 | tf_op jit(solution)/shard_map/all_to_all | solution.py:73
  215.5 2.0 gather_fusion.8
  217.5 2.1 gather_fusion.9
  219.6 8.7 %all-to-all-done.2 = bf16[8,32,2048]{2,1,0:T(8,128)(2,1)S(1)} async-done(((bf16[8,32,2048]{2,1,0:T(8,128)(2,1)}), bf16[8,32,2048]{2,1,0:T(8,128)(2,1)S(1)}, u32[]{:S(2)}, u32[]{:S(2)}) %all-to-all-start.2) | async-done | bytes 1048608 | tf_op jit(solution)/shard_map/all_to_all | solution.py:73
  228.3 2.0 gather_fusion.1
  230.3 2.0 gather_fusion.2
  232.3 2.1 gather_fusion.10
  234.4 2.0 gather_fusion.3
  236.4 2.0 gather_fusion.11
  238.5 2.0 gather_fusion.4
  240.5 2.0 gather_fusion.12
  242.5 2.1 gather_fusion.5
  244.6 2.0 gather_fusion.13
  246.6 2.0 gather_fusion.6
  248.7 3.9 add_convert_fusion
  252.6 1.9 add_convert_fusion.1
  254.5 20.4 %reduce-scatter.6.cloned.1.call-done = bf16[64,768]{1,0:T(8,128)(2,1)} async-done(((bf16[2048,768]{1,0:T(8,128)(2,1)}), bf16[64,768]{1,0:T(8,128)(2,1)}) %reduce-scatter.6.cloned.1.call-update) | async-done | bytes 98320 | tf_op jit(solution)/shard_map/reduce_scatter | solution.py:95
  274.9 1.6 bitcast_convert_fusion.1
  276.5 95.9 %reduce-scatter.4.cloned.1.call-done = bf16[64,768]{1,0:T(8,128)(2,1)} async-done(((bf16[2048,768]{1,0:T(8,128)(2,1)}), bf16[64,768]{1,0:T(8,128)(2,1)}) %reduce-scatter.4.cloned.1.call-update) | async-done | bytes 98320 | tf_op jit(solution)/shard_map/reduce_scatter | solution.py:92
  372.4 1.6 bitcast_convert_fusion.2
  374.0 95.3 %reduce-scatter.8.cloned.1.call-done = bf16[64,768]{1,0:T(8,128)(2,1)} async-done(((bf16[2048,768]{1,0:T(8,128)(2,1)}), bf16[64,768]{1,0:T(8,128)(2,1)}) %reduce-scatter.8.cloned.1.call-update) | async-done | bytes 98320 | tf_op jit(solution)/shard_map/reduce_scatter | solution.py:98
  469.3 1.6 bitcast_convert_fusion
  (74 shorter events, 4.9 us)
Async XLA Ops:
  7.2 7.3 %copy-start = (bf16[192,2048]{1,0:T(8,128)(2,1)S(1)}, bf16[192,2048]{1,0:T(8,128)(2,1)}, u32[]{:S(2)}) copy-start(bf16[192,2048]{1,0:T(8,128)(2,1)} %param.13) | copy-start | bytes 2359300
  7.2 160.5 %all-gather.5.cloned.1.call-start = ((), (), s32[]{:S(2)}) async-start(), calls=%async_computation.9 | async-start | bytes 3244032 | tf_op jit(solution)/shard_map/all_gather | solution.py:41
  16.2 22.2 %copy-start.14 = (bf16[1,64,768]{2,1,0:T(8,128)(2,1)S(1)}, bf16[1,64,768]{2,1,0:T(8,128)(2,1)}, u32[]{:S(2)}) copy-start(bf16[1,64,768]{2,1,0:T(8,128)(2,1)} %param.12) | copy-start | bytes 294916
  40.3 12.7 %copy-start.1 = (bf16[192,2048]{1,0:T(8,128)(2,1)S(1)}, bf16[192,2048]{1,0:T(8,128)(2,1)}, u32[]{:S(2)}) copy-start(bf16[192,2048]{1,0:T(8,128)(2,1)} %param.7) | copy-start | bytes 2359300
  40.3 98.5 %all-to-all-start.1 = ((bf16[32,1,64,768]{3,2,1,0:T(8,128)(2,1)}), bf16[32,1,64,768]{3,2,1,0:T(8,128)(2,1)}, u32[]{:S(2)}, u32[]{:S(2)}) async-start(bf16[32,1,64,768]{3,2,1,0:T(8,128)(2,1)} %stack.2), calls=%async_computation.1 | async-start | bytes 6291456 | tf_op jit(solution)/shard_map/all_to_all | solution.py:43
  52.2 121.2 %all-gather.3.cloned.1.call-start = ((), (), s32[]{:S(2)}) async-start(), calls=%async_computation.8 | async-start | bytes 3244032 | tf_op jit(solution)/shard_map/all_gather | solution.py:40
  138.8 28.8 %all-to-all-start = ((bf16[8,32,2048]{2,1,0:T(8,128)(2,1)}), bf16[8,32,2048]{2,1,0:T(8,128)(2,1)S(1)}, u32[]{:S(2)}, u32[]{:S(2)}) async-start(bf16[8,32,2048]{2,1,0:T(8,128)(2,1)} %broadcast_select_fusion), calls=%async_computation | async-start | bytes 2097152 | tf_op jit(solution)/shard_map/all_to_all | solution.py:47
  144.7 130.2 %reduce-scatter.6.cloned.1.call-start = ((), (), s32[]{:S(2)}) async-start(), calls=%async_computation.11 | async-start | bytes 3244032 | tf_op jit(solution)/shard_map/reduce_scatter | solution.py:95
  177.7 0.7 copy-start.11
  181.2 191.2 %reduce-scatter.4.cloned.1.call-start = ((), (), s32[]{:S(2)}) async-start(), calls=%async_computation.10 | async-start | bytes 3244032 | tf_op jit(solution)/shard_map/reduce_scatter | solution.py:92
  184.0 1.0 copy-start.12
  185.0 3.1 copy-start.2
  190.1 5.3 %copy-start.13 = (bf16[256,768]{1,0:T(8,128)(2,1)S(1)}, bf16[256,768]{1,0:T(8,128)(2,1)}, u32[]{:S(2)}) copy-start(bf16[256,768]{1,0:T(8,128)(2,1)} %get-tuple-element.16) | copy-start | bytes 1179652
  190.1 19.4 %all-to-all-start.4 = ((bf16[8,32,2048]{2,1,0:T(8,128)(2,1)}), bf16[8,32,2048]{2,1,0:T(8,128)(2,1)S(1)}, u32[]{:S(2)}, u32[]{:S(2)}) async-start(bf16[8,32,2048]{2,1,0:T(8,128)(2,1)} %bitcast.101), calls=%async_computation.4 | async-start | bytes 2097152 | tf_op jit(solution)/shard_map/all_to_all | solution.py:80
  195.4 273.9 %reduce-scatter.8.cloned.1.call-start = ((), (), s32[]{:S(2)}) async-start(), calls=%async_computation.12 | async-start | bytes 3244032 | tf_op jit(solution)/shard_map/reduce_scatter | solution.py:98
  202.2 13.1 %copy-start.15 = (s32[192,6]{0,1:T(8,128)S(1)}, s32[192,6]{0,1:T(8,128)}, u32[]{:S(2)}) copy-start(s32[192,6]{0,1:T(8,128)} %param.8) | copy-start | bytes 13828
  209.5 18.8 %all-to-all-start.2 = ((bf16[8,32,2048]{2,1,0:T(8,128)(2,1)}), bf16[8,32,2048]{2,1,0:T(8,128)(2,1)S(1)}, u32[]{:S(2)}, u32[]{:S(2)}) async-start(bf16[8,32,2048]{2,1,0:T(8,128)(2,1)} %bitcast.104), calls=%async_computation.2 | async-start | bytes 2097152 | tf_op jit(solution)/shard_map/all_to_all | solution.py:73
  246.6 2.0 copy-start.7
  246.6 2.0 copy-start.8
  248.6 4.0 copy-start.3
  248.6 4.0 copy-start.4
  248.6 4.0 copy-start.5
  248.6 4.0 copy-start.6
  248.7 4.0 copy-start.9
  248.7 4.0 copy-start.10
Sparse Core Ops, SparseCore 0:
  10.6 75.0 all-gather.4
  88.1 85.2 all-gather.2
  181.3 93.5 reduce-scatter.5
  279.2 93.1 reduce-scatter.3
  376.1 93.1 reduce-scatter.7
